TPU v7x, 128 devices: a whole 4x4x4 slice. The times are simulated.
128 devices in a mesh: rep: 4 (over z_lo, core), ep: 32 (over y, x, z_hi).
Axes of the slice: x: 4, y: 4, z: 4 (z_hi: 2, z_lo: 2; z = z_hi * 2 + z_lo), core: 2. Of those that a mesh axis runs over, the one named last changes fastest.
Arguments:
- tokens: bfloat16 [16384, 2048], P(('rep', 'ep')), may hold values from -6 to 6
- expert_ids: int32 [16384, 8], P(('rep', 'ep')), may hold values from 0 to 127, as said below
- route_weight: float32 [16384, 8], P(('rep', 'ep')), may hold values from 0.05 to 1
- hot_plan: int32 [32], replicated, may hold values from 0 to 3, as said below
- gate_proj: bfloat16 [128, 2048, 768], P(('rep', 'ep')), may hold values from -0.125 to 0.125
- up_proj: bfloat16 [128, 2048, 768], P(('rep', 'ep')), may hold values from -0.125 to 0.125
- down_proj: bfloat16 [128, 768, 2048], P(('rep', 'ep')), may hold values from -0.21875 to 0.21875
Outputs:
- layer_out: bfloat16 [16384, 2048], P(('rep', 'ep'))
- served_load: float32 [128], replicated
Inputs may be any that keep to these rules, and one draw needn't show every extreme that they name: `expert_ids`: within the rows of one device (aligned blocks of 128 tokens) a hot expert is named at most 16 times and any other expert at most 6 times. Some expert that is not hot is named exactly 6 times in every block, and the hot expert of some column exactly 16 times in every block. Expert hot_plan[c] * 32 + c is the hot expert of column c.
All inputs are finite; a program needn't handle non-finite values.
Results may differ from a plain program's by a relative error of at most 0.0057.
Values may be sent and summed in bfloat16 or wider, within the bound.
No kernel may reach another device: no remote copies, remote signals or barrier semaphores. Data moves between devices by JAX's collectives and lax.ppermute only.
A program may use at most 128 MiB of HBM per device.

v0:
```python
import jax
import jax.numpy as jnp
from jax import lax
from jax.sharding import PartitionSpec as P


def from_root(array, axis, root):
    mine = lax.axis_index(axis) == root
    return lax.psum(jnp.where(mine, array, jnp.zeros_like(array)), axis)


def expert_ffn(slot_rows, gate_mat, up_mat, down_mat):
    layout = slot_rows.shape
    flattened = slot_rows.reshape(-1, layout[-1])
    gate_in = jnp.dot(flattened, gate_mat, preferred_element_type=jnp.float32)
    up_in = jnp.dot(flattened, up_mat, preferred_element_type=jnp.float32)
    hidden = (jax.nn.silu(gate_in) * up_in).astype(jnp.bfloat16)
    result = jnp.dot(hidden, down_mat, preferred_element_type=jnp.float32).astype(jnp.bfloat16)
    return result.reshape(layout)


def local(tokens, expert_ids, route_weight, hot_plan, gate_proj, up_proj, down_proj):
    n_rep = lax.axis_size("rep")
    n_ep = lax.axis_size("ep")
    devices = n_rep * n_ep
    my_row = lax.axis_index("rep")
    my_col = lax.axis_index("ep")
    tok_rows, top_count = expert_ids.shape
    model_width = tokens.shape[1]
    routed = tok_rows * top_count
    cool_cap = max(2, 3 * routed // (4 * devices))
    hot_cap = max(4, 2 * routed // devices)
    flat_ids = expert_ids.reshape(-1)
    expert_range = jnp.arange(devices, dtype=jnp.int32)
    column_range = jnp.arange(n_ep, dtype=jnp.int32)
    one_hot = (flat_ids[:, None] == expert_range[None, :]).astype(jnp.int32)
    own_counts = jnp.sum(one_hot, axis=0, dtype=jnp.int32)
    row_match = (jnp.arange(n_rep, dtype=jnp.int32) == my_row)[:, None]
    placed = jnp.where(row_match, own_counts[None, :], jnp.zeros_like(own_counts)[None, :])
    row_counts = lax.psum(placed, ("rep", "ep"))
    same_column = expert_range[:, None] % n_ep == column_range[None, :]
    same_row = expert_range[:, None] // n_ep == hot_plan[None, :]
    hot_flag = jnp.any(same_column & same_row, axis=1)
    counts = jnp.sum(row_counts, axis=0, dtype=jnp.int32)
    hot_expert = hot_plan * n_ep + column_range
    copy_rows = row_counts[:, hot_expert].reshape(-1)
    served = jnp.where(hot_flag, jnp.zeros_like(counts), counts) + copy_rows
    served_load = served.astype(jnp.float32) / jnp.float32(routed)
    is_hot = jnp.sum(one_hot * hot_flag.astype(jnp.int32)[None, :], axis=1, dtype=jnp.int32) > 0
    ordinal = jnp.sum((jnp.cumsum(one_hot, axis=0) - 1) * one_hot, axis=1)
    home_col = flat_ids % n_ep
    source = jnp.arange(routed, dtype=jnp.int32) // top_count

    def pack_rows(slot, total):
        owners = jnp.zeros((total + 1,), jnp.int32).at[slot].set(source)[:total]
        filled = jnp.zeros((total + 1,), jnp.bool_).at[slot].set(True)[:total]
        return jnp.where(filled[:, None], tokens[owners], jnp.zeros((), jnp.bfloat16))

    home_total = devices * cool_cap
    home_slot = jnp.where(is_hot, home_total, flat_ids * cool_cap + ordinal)
    copy_total = n_ep * hot_cap
    copy_slot = jnp.where(is_hot, home_col * hot_cap + ordinal, copy_total)
    copy_send = pack_rows(copy_slot, copy_total).reshape(n_ep, hot_cap, model_width)
    copied = (
        from_root(gate_proj[0], "rep", hot_plan[my_col]),
        from_root(up_proj[0], "rep", hot_plan[my_col]),
        from_root(down_proj[0], "rep", hot_plan[my_col]),
    )
    copy_done = expert_ffn(
        lax.all_to_all(copy_send, "ep", split_axis=0, concat_axis=0, tiled=True),
        copied[0],
        copied[1],
        copied[2],
    )
    copy_back = lax.all_to_all(copy_done, "ep", split_axis=0, concat_axis=0, tiled=True)
    copy_result = copy_back.reshape(copy_total, model_width)[jnp.minimum(copy_slot, copy_total - 1)]
    home_send = pack_rows(home_slot, home_total).reshape(devices, cool_cap, model_width)
    home_done = expert_ffn(
        lax.all_to_all(home_send, ("rep", "ep"), split_axis=0, concat_axis=0, tiled=True),
        gate_proj[0],
        up_proj[0],
        down_proj[0],
    )
    home_back = lax.all_to_all(home_done, ("rep", "ep"), split_axis=0, concat_axis=0, tiled=True)
    home_result = home_back.reshape(home_total, model_width)[jnp.minimum(home_slot, home_total - 1)]
    gathered = jnp.where(is_hot[:, None], copy_result, home_result)
    shares = route_weight / jnp.sum(route_weight, axis=1, keepdims=True)
    combined = jnp.sum(
        shares[:, :, None] * gathered.reshape(tok_rows, top_count, model_width).astype(jnp.float32),
        axis=1,
    )
    return (combined.astype(jnp.bfloat16), served_load)


def solution(mesh):
    placed = (
        P(("rep", "ep"), None),
        P(("rep", "ep"), None),
        P(("rep", "ep"), None),
        P(),
        P(("rep", "ep"), None, None),
        P(("rep", "ep"), None, None),
        P(("rep", "ep"), None, None),
    )
    return jax.shard_map(
        local, mesh=mesh, in_specs=placed, out_specs=(P(("rep", "ep"), None), P()), check_vma=False
    )
```

profile of v0, /device:TPU:1, one launch (start us, length us, event | category | flops | bytes accessed | tf_op | source)
XLA Modules:
  0.0 456.8 jit_solution(834048434750761366)
XLA Ops:
  7.2 0.0 copy-start
  7.2 0.0 all-reduce.3.cloned.1.call-start
  7.2 1.3 dynamic_slice.2
  9.2 0.0 copy-start.2
  9.2 0.0 copy-start.3
  9.2 3.9 bitcast_select_fusion.1
  13.1 0.0 copy-done.2
  13.1 1.0 copy-done.3
  14.1 3.0 bitcast_select_fusion.2
  17.1 0.0 copy-start.5
  17.1 0.0 all-reduce.3.cloned.1.call-update
  17.2 0.7 copy-done.5
  17.8 0.1 copy.19
  17.9 0.1 eq.80
  18.0 0.1 copy.22
  18.1 0.2 fusion.10
  18.3 0.1 eq.70
  18.4 0.1 reshape.309
  18.6 0.1 copy.23
  18.7 0.0 copy-done.6
  18.7 0.1 fusion.14
  18.8 0.5 convert_reduce_fusion
  19.4 4.3 scatter_custom_fusion.3
  23.8 0.0 copy-done
  23.8 4.4 gather_fusion.2
  28.1 6.3 %gather.28 = bf16[128,6,2048]{2,1,0:T(8,128)(2,1)} reshape(bf16[768,2048]{1,0:T(8,128)(2,1)} %gather_fusion.2) | data formatting | bytes 6291456 | tf_op jit(solution)/shard_map/gather | solution.py:57
  34.4 4.3 scatter_custom_fusion.2
  38.8 0.2 broadcast_in_dim.123
  39.0 4.7 %broadcast_select_fusion = bf16[128,6,2048]{2,1,0:T(8,128)(2,1)} fusion(bf16[128,6,2048]{2,1,0:T(8,128)(2,1)} %gather.28, pred[128,6]{1,0:T(8,128)(4,1)S(1)} %broadcast_in_dim.123), kind=kLoop, calls=%fused_computation.11 | loop fusion | flops 1572864 | bytes 6292224 | tf_op jit(solution)/shard_map/jit(_where)/select_n | solution.py:57
  43.7 11.8 %all-to-all-start.2 = ((bf16[128,6,2048]{2,1,0:T(8,128)(2,1)}), bf16[128,6,2048]{2,1,0:T(8,128)(2,1)}, u32[]{:S(2)}, u32[]{:S(2)}) async-start(bf16[128,6,2048]{2,1,0:T(8,128)(2,1)} %broadcast_select_fusion), calls=%async_computation.2 | async-start | bytes 8388608 | tf_op jit(solution)/shard_map/all_to_all | solution.py:79
  55.6 4.5 scatter_custom_fusion.1
  60.1 4.3 scatter_custom_fusion
  64.4 2.5 gather_fusion
  66.9 0.1 broadcast_in_dim.115
  67.0 1.6 broadcast_select_fusion.1
  68.6 39.2 %all-to-all-done.2 = bf16[128,6,2048]{2,1,0:T(8,128)(2,1)} async-done(((bf16[128,6,2048]{2,1,0:T(8,128)(2,1)}), bf16[128,6,2048]{2,1,0:T(8,128)(2,1)}, u32[]{:S(2)}, u32[]{:S(2)}) %all-to-all-start.2) | async-done | bytes 3145760 | tf_op jit(solution)/shard_map/all_to_all | solution.py:79
  107.8 7.8 %all-to-all-start = ((bf16[32,16,2048]{2,1,0:T(8,128)(2,1)}), bf16[32,16,2048]{2,1,0:T(8,128)(2,1)S(1)}, u32[]{:S(2)}, u32[]{:S(2)}) async-start(bf16[32,16,2048]{2,1,0:T(8,128)(2,1)} %broadcast_select_fusion.1), calls=%async_computation | async-start | bytes 4194304 | tf_op jit(solution)/shard_map/all_to_all | solution.py:70
  115.5 6.4 %reshape.314 = bf16[768,2048]{1,0:T(8,128)(2,1)} reshape(bf16[128,6,2048]{2,1,0:T(8,128)(2,1)} %all-to-all-done.2) | data formatting | bytes 6291456 | tf_op jit(solution)/shard_map/reshape | solution.py:14
  121.9 7.0 %fusion.1 = f32[768,768]{1,0:T(8,128)} fusion(bf16[768,2048]{1,0:T(8,128)(2,1)} %reshape.314, bf16[1,2048,768]{2,1,0:T(8,128)(2,1)} %param.12), kind=kOutput, calls=%fused_computation.15 | convolution fusion | flops 2415919104 | bytes 8650752 | tf_op jit(solution)/shard_map/dot_general | solution.py:16
  128.9 12.0 %convolution_convert_fusion = bf16[768,2048]{1,0:T(8,128)(2,1)} fusion(bf16[1,768,2048]{2,1,0:T(8,128)(2,1)} %param.13, f32[768,768]{1,0:T(8,128)} %fusion.1, bf16[768,2048]{1,0:T(8,128)(2,1)} %reshape.314, bf16[1,2048,768]{2,1,0:T(8,128)(2,1)} %param.11), kind=kOutput, calls=%fused_computation.12 | convolution fusion | flops 4836950016 | bytes 14942208 | tf_op jit(solution)/shard_map/dot_general | solution.py:18
  140.9 6.3 %reshape.315 = bf16[128,6,2048]{2,1,0:T(8,128)(2,1)} reshape(bf16[768,2048]{1,0:T(8,128)(2,1)} %convolution_convert_fusion) | data formatting | bytes 6291456 | tf_op jit(solution)/shard_map/reshape | solution.py:19
  147.2 0.0 all-to-all-done
  147.2 10.1 %all-to-all-start.3 = ((bf16[128,6,2048]{2,1,0:T(8,128)(2,1)}), bf16[128,6,2048]{2,1,0:T(8,128)(2,1)}, u32[]{:S(2)}, u32[]{:S(2)}) async-start(bf16[128,6,2048]{2,1,0:T(8,128)(2,1)} %reshape.315), calls=%async_computation.3 | async-start | bytes 8388608 | tf_op jit(solution)/shard_map/all_to_all | solution.py:84
  157.3 153.7 %all-reduce.3.cloned.1.call-done = (bf16[768,2048]{1,0:T(8,128)(2,1)}, bf16[2048,768]{1,0:T(8,128)(2,1)}, bf16[2048,768]{1,0:T(8,128)(2,1)}) async-done(((bf16[768,2048]{1,0:T(8,128)(2,1)}, bf16[2048,768]{1,0:T(8,128)(2,1)}, bf16[2048,768]{1,0:T(8,128)(2,1)}), (bf16[768,2048]{1,0:T(8,128)(2,1)}, bf16[2048,768]{1,0:T(8,128)(2,1)}, bf16[2048,768]{1,0:T(8,128)(2,1)})) %all-reduce.3.cloned.1.call-update) | async-done | bytes 9437200 | tf_op jit(solution)/shard_map/psum | solution.py:9
  311.0 4.8 %fusion.31 = f32[512,768]{1,0:T(8,128)} fusion(bf16[512,2048]{1,0:T(8,128)(2,1)S(1)} %bitcast.52, bf16[2048,768]{1,0:T(8,128)(2,1)} %get-tuple-element.6), kind=kOutput, calls=%fused_computation.86 | convolution fusion | flops 1610612736 | bytes 6815744 | tf_op jit(solution)/shard_map/dot_general | solution.py:15
  315.8 8.6 %convolution_convert_fusion.1 = bf16[512,2048]{1,0:T(8,128)(2,1)} fusion(bf16[768,2048]{1,0:T(8,128)(2,1)} %get-tuple-element.5, f32[512,768]{1,0:T(8,128)} %fusion.31, bf16[512,2048]{1,0:T(8,128)(2,1)S(1)} %bitcast.53, bf16[2048,768]{1,0:T(8,128)(2,1)} %get-tuple-element.7), kind=kOutput, calls=%fused_computation.21 | convolution fusion | flops 3224633344 | bytes 12058624 | tf_op jit(solution)/shard_map/dot_general | solution.py:18
  324.4 0.0 all-to-all-done.3
  324.4 9.5 %all-to-all-start.1 = ((bf16[32,16,2048]{2,1,0:T(8,128)(2,1)}), bf16[32,16,2048]{2,1,0:T(8,128)(2,1)S(1)}, u32[]{:S(2)}, u32[]{:S(2)}) async-start(bf16[32,16,2048]{2,1,0:T(8,128)(2,1)} %bitcast.51), calls=%async_computation.1 | async-start | bytes 4194304 | tf_op jit(solution)/shard_map/all_to_all | solution.py:75
  333.9 0.1 gt.32
  334.0 0.0 copy-done.4
  334.1 0.1 copy.18
  334.2 0.1 broadcast_select_fusion.2
  334.3 83.8 %psum.31 = s32[4,128]{0,1:T(8,128)S(1)} all-reduce(s32[4,128]{0,1:T(8,128)S(1)} %broadcast_select_fusion.2), channel_id=1, replica_groups=mesh['rep'=4,'ep'=32] {'rep','ep'}, use_global_device_ids=true, to_apply=%region_15.16 | all-reduce | flops 512 | bytes 4096 | tf_op jit(solution)/shard_map/psum | solution.py:40
  418.1 0.1 reduce_sum.62
  418.2 0.6 gather_fusion.4
  418.8 0.1 copy.24
  418.9 0.1 reshape.317
  419.0 0.5 convert_multiply_fusion
  419.5 6.3 %reshape.316 = bf16[768,2048]{1,0:T(8,128)(2,1)} reshape(bf16[128,6,2048]{2,1,0:T(8,128)(2,1)} %all-to-all-done.3) | data formatting | bytes 6291456 | tf_op jit(solution)/shard_map/reshape | solution.py:85
  425.8 11.1 %gather_fusion.3 = bf16[1024,2048]{1,0:T(8,128)(2,1)} fusion(bf16[768,2048]{1,0:T(8,128)(2,1)} %reshape.316, s32[1024]{0:T(1024)S(1)} %broadcast_clamp_fusion), kind=kCustom, calls=%fused_computation.3 | custom fusion | bytes 8392704 | tf_op jit(solution)/shard_map/gather | solution.py:85
  436.9 0.0 all-to-all-done.1
  437.0 6.0 %gather_fusion.1 = bf16[1024,2048]{1,0:T(8,128)(2,1)} fusion(bf16[512,2048]{1,0:T(8,128)(2,1)S(1)} %bitcast.49, s32[1024]{0:T(1024)S(1)} %broadcast_clamp_fusion.1), kind=kCustom, calls=%fused_computation.1 | custom fusion | bytes 8392704 | tf_op jit(solution)/shard_map/gather | solution.py:76
  443.0 7.0 %multiply_reduce_fusion = bf16[128,2048]{1,0:T(8,128)(2,1)} fusion(bf16[1024,2048]{1,0:T(8,128)(2,1)} %gather_fusion.3, bf16[1024,2048]{1,0:T(8,128)(2,1)} %gather_fusion.1, f32[128,8]{1,0:T(8,128)S(1)} %copy.18, pred[128,8]{1,0:T(8,128)(4,1)S(1)} %gt.32), kind=kLoop, calls=%fused_computation.9 | loop fusion | flops 8126464 | bytes 8918016 | tf_op jit(solution)/shard_map/reduce_sum | solution.py:88
  450.0 0.0 copy-done.1
  (27 shorter events, 0.2 us)
Async XLA Ops:
  7.2 16.6 %copy-start = (bf16[128,2048]{1,0:T(8,128)(2,1)S(1)}, bf16[128,2048]{1,0:T(8,128)(2,1)}, u32[]{:S(2)}) copy-start(bf16[128,2048]{1,0:T(8,128)(2,1)} %param.7) | copy-start | bytes 1572868
  7.2 303.8 %all-reduce.3.cloned.1.call-start = ((), (), s32[]{:S(2)}) async-start(), calls=%async_computation.4 | async-start | bytes 18874368 | tf_op jit(solution)/shard_map/psum | solution.py:9
  9.2 3.9 copy-start.2
  9.2 4.9 %copy-start.3 = (bf16[1,2048,768]{2,1,0:T(8,128)(2,1)S(1)}, bf16[1,2048,768]{2,1,0:T(8,128)(2,1)}, u32[]{:S(2)}) copy-start(bf16[1,2048,768]{2,1,0:T(8,128)(2,1)} %param.11) | copy-start | bytes 9437188
  17.1 0.7 copy-start.5
  17.1 1.6 copy-start.6
  43.7 64.1 %all-to-all-start.2 = ((bf16[128,6,2048]{2,1,0:T(8,128)(2,1)}), bf16[128,6,2048]{2,1,0:T(8,128)(2,1)}, u32[]{:S(2)}, u32[]{:S(2)}) async-start(bf16[128,6,2048]{2,1,0:T(8,128)(2,1)} %broadcast_select_fusion), calls=%async_computation.2 | async-start | bytes 8388608 | tf_op jit(solution)/shard_map/all_to_all | solution.py:79
  107.8 39.4 %all-to-all-start = ((bf16[32,16,2048]{2,1,0:T(8,128)(2,1)}), bf16[32,16,2048]{2,1,0:T(8,128)(2,1)S(1)}, u32[]{:S(2)}, u32[]{:S(2)}) async-start(bf16[32,16,2048]{2,1,0:T(8,128)(2,1)} %broadcast_select_fusion.1), calls=%async_computation | async-start | bytes 4194304 | tf_op jit(solution)/shard_map/all_to_all | solution.py:70
  147.2 177.3 %all-to-all-start.3 = ((bf16[128,6,2048]{2,1,0:T(8,128)(2,1)}), bf16[128,6,2048]{2,1,0:T(8,128)(2,1)}, u32[]{:S(2)}, u32[]{:S(2)}) async-start(bf16[128,6,2048]{2,1,0:T(8,128)(2,1)} %reshape.315), calls=%async_computation.3 | async-start | bytes 8388608 | tf_op jit(solution)/shard_map/all_to_all | solution.py:84
  324.4 9.6 %copy-start.4 = (f32[128,8]{0,1:T(8,128)S(1)}, f32[128,8]{0,1:T(8,128)}, u32[]{:S(2)}) copy-start(f32[128,8]{0,1:T(8,128)} %param.9) | copy-start | bytes 12292
  324.4 112.5 %all-to-all-start.1 = ((bf16[32,16,2048]{2,1,0:T(8,128)(2,1)}), bf16[32,16,2048]{2,1,0:T(8,128)(2,1)S(1)}, u32[]{:S(2)}, u32[]{:S(2)}) async-start(bf16[32,16,2048]{2,1,0:T(8,128)(2,1)} %bitcast.51), calls=%async_computation.1 | async-start | bytes 4194304 | tf_op jit(solution)/shard_map/all_to_all | solution.py:75
  436.9 13.0 %copy-start.1 = (bf16[128,2048]{1,0:T(8,128)(2,1)S(1)}, bf16[128,2048]{1,0:T(8,128)(2,1)}, u32[]{:S(2)}) copy-start(bf16[128,2048]{1,0:T(8,128)(2,1)} %param.7) | copy-start | bytes 1572868
Sparse Core Ops, SparseCore 0:
  17.3 293.6 all-reduce.2
where the time goes:
time: 458 us; the launch traced here: 457 us
  waiting for transfers between devices  193 us (42%)
  blocking collectives  83.8 us (18%)
  local copies, waits for them, and re-layouts  71.5 us (16%)
  starting transfers between devices  39.2 us (9%)
  matrix products  32.5 us (7%)
  other arithmetic  21.9 us (5%)
  between operations  15 us (3%)
    psum x1, waiting for transfers between devices, from_root(): return lax.psum(jnp.where(mine, array, jnp.zeros_like(array)), axis)  154 us
    psum x1, blocking collectives, local(): row_counts = lax.psum(placed, ('rep', 'ep'))  83.8 us
    all_to_all x1, waiting for transfers between devices, local(): lax.all_to_all(home_send, ('rep', 'ep'), split_axis=0, concat_axis=0, til...  39.2 us
    dot_general x2, matrix products, expert_ffn(): jnp.dot(hidden, down_mat, preferred_element_type=jnp.float32)  20.7 us
    gather x3, local copies, waits for them, and re-layouts, pack_rows(): tokens[owners]  13.1 us
    all_to_all x1, starting transfers between devices, local(): lax.all_to_all(home_send, ('rep', 'ep'), split_axis=0, concat_axis=0, til...  11.8 us
    gather x1, local copies, waits for them, and re-layouts, local(): home_back.reshape(home_total, model_width)  11.1 us
    all_to_all x1, starting transfers between devices, local(): lax.all_to_all(home_done, ('rep', 'ep'), split_axis=0, concat_axis=0, til...  10.1 us
  transfers between devices with their start and end apart: 5, of which 2 were waited for; matrix products, arithmetic and copies ran while one was open for 23% of the time, Pallas kernels for 0%

commit v1 on v0

--- a/solution.py
+++ b/solution.py
@@ -37,7 +37,7 @@
     own_counts = jnp.sum(one_hot, axis=0, dtype=jnp.int32)
     row_match = (jnp.arange(n_rep, dtype=jnp.int32) == my_row)[:, None]
     placed = jnp.where(row_match, own_counts[None, :], jnp.zeros_like(own_counts)[None, :])
-    row_counts = lax.psum(placed, ("rep", "ep"))
+    row_counts = lax.psum(lax.psum(placed, "rep"), "ep")
     same_column = expert_range[:, None] % n_ep == column_range[None, :]
     same_row = expert_range[:, None] // n_ep == hot_plan[None, :]
     hot_flag = jnp.any(same_column & same_row, axis=1)

time: 458 us -> 587 us (1.28)
  the two profiles are of different devices: /device:TPU:1 before, /device:TPU:0 now
where the time goes in v1:
time: 587 us; the launch traced here: 586 us
  blocking collectives  214 us (36%)
  waiting for transfers between devices  191 us (33%)
  local copies, waits for them, and re-layouts  71.6 us (12%)
  starting transfers between devices  40.4 us (7%)
  matrix products  32.4 us (6%)
  other arithmetic  21.9 us (4%)
  between operations  15 us (3%)
    psum x2, blocking collectives, local(): row_counts = lax.psum(lax.psum(placed, 'rep'), 'ep')  214 us
    psum x1, waiting for transfers between devices, from_root(): return lax.psum(jnp.where(mine, array, jnp.zeros_like(array)), axis)  153 us
    all_to_all x1, waiting for transfers between devices, local(): lax.all_to_all(home_send, ('rep', 'ep'), split_axis=0, concat_axis=0, til...  38 us
    dot_general x2, matrix products, expert_ffn(): jnp.dot(hidden, down_mat, preferred_element_type=jnp.float32)  20.6 us
    gather x3, local copies, waits for them, and re-layouts, pack_rows(): tokens[owners]  13.2 us
  transfers between devices with their start and end apart: 5, of which 2 were waited for; matrix products, arithmetic and copies ran while one was open for 18% of the time, Pallas kernels for 0%

profile of v1, /device:TPU:0, one launch (start us, length us, event | category | flops | bytes accessed | tf_op | source)
XLA Modules:
  0.0 585.5 jit_solution(13967426779845397310)
XLA Ops:
  7.2 0.0 copy-start
  7.2 0.0 all-reduce.3.cloned.1.call-start
  7.2 1.3 dynamic_slice.2
  9.2 0.0 copy-start.2
  9.2 0.0 copy-start.3
  9.2 3.9 bitcast_select_fusion.1
  13.1 0.0 copy-done.2
  13.1 1.0 copy-done.3
  14.1 3.0 bitcast_select_fusion.2
  17.1 0.0 all-reduce.3.cloned.1.call-update
  17.2 0.7 copy-done.5
  17.8 0.1 copy.19
  17.9 0.1 eq.80
  18.0 0.1 copy.22
  18.1 0.2 fusion.10
  18.3 0.1 eq.70
  18.4 0.1 reshape.309
  18.6 0.1 copy.23
  18.7 0.0 copy-done.6
  18.7 0.1 fusion.14
  18.8 0.5 convert_reduce_fusion
  19.4 4.3 scatter_custom_fusion.3
  23.8 0.0 copy-done
  23.8 4.4 gather_fusion.2
  28.1 6.4 %gather.28 = bf16[128,6,2048]{2,1,0:T(8,128)(2,1)} reshape(bf16[768,2048]{1,0:T(8,128)(2,1)} %gather_fusion.2) | data formatting | bytes 6291456 | tf_op jit(solution)/shard_map/gather | solution.py:57
  34.5 4.3 scatter_custom_fusion.2
  38.9 0.2 broadcast_in_dim.123
  39.0 4.7 broadcast_select_fusion
  43.7 11.6 %all-to-all-start.2 = ((bf16[128,6,2048]{2,1,0:T(8,128)(2,1)}), bf16[128,6,2048]{2,1,0:T(8,128)(2,1)}, u32[]{:S(2)}, u32[]{:S(2)}) async-start(bf16[128,6,2048]{2,1,0:T(8,128)(2,1)} %broadcast_select_fusion), calls=%async_computation.2 | async-start | bytes 8388608 | tf_op jit(solution)/shard_map/all_to_all | solution.py:79
  55.3 4.5 scatter_custom_fusion.1
  59.8 4.3 scatter_custom_fusion
  64.2 2.5 gather_fusion
  66.7 0.1 broadcast_in_dim.115
  66.8 1.6 broadcast_select_fusion.1
  68.3 38.0 %all-to-all-done.2 = bf16[128,6,2048]{2,1,0:T(8,128)(2,1)} async-done(((bf16[128,6,2048]{2,1,0:T(8,128)(2,1)}), bf16[128,6,2048]{2,1,0:T(8,128)(2,1)}, u32[]{:S(2)}, u32[]{:S(2)}) %all-to-all-start.2) | async-done | bytes 3145760 | tf_op jit(solution)/shard_map/all_to_all | solution.py:79
  106.3 8.5 %all-to-all-start = ((bf16[32,16,2048]{2,1,0:T(8,128)(2,1)}), bf16[32,16,2048]{2,1,0:T(8,128)(2,1)S(1)}, u32[]{:S(2)}, u32[]{:S(2)}) async-start(bf16[32,16,2048]{2,1,0:T(8,128)(2,1)} %broadcast_select_fusion.1), calls=%async_computation | async-start | bytes 4194304 | tf_op jit(solution)/shard_map/all_to_all | solution.py:70
  114.9 6.4 %reshape.314 = bf16[768,2048]{1,0:T(8,128)(2,1)} reshape(bf16[128,6,2048]{2,1,0:T(8,128)(2,1)} %all-to-all-done.2) | data formatting | bytes 6291456 | tf_op jit(solution)/shard_map/reshape | solution.py:14
  121.2 7.0 %fusion.1 = f32[768,768]{1,0:T(8,128)} fusion(bf16[768,2048]{1,0:T(8,128)(2,1)} %reshape.314, bf16[1,2048,768]{2,1,0:T(8,128)(2,1)} %param.12), kind=kOutput, calls=%fused_computation.15 | convolution fusion | flops 2415919104 | bytes 8650752 | tf_op jit(solution)/shard_map/dot_general | solution.py:16
  128.2 12.0 %convolution_convert_fusion = bf16[768,2048]{1,0:T(8,128)(2,1)} fusion(bf16[1,768,2048]{2,1,0:T(8,128)(2,1)} %param.13, f32[768,768]{1,0:T(8,128)} %fusion.1, bf16[768,2048]{1,0:T(8,128)(2,1)} %reshape.314, bf16[1,2048,768]{2,1,0:T(8,128)(2,1)} %param.11), kind=kOutput, calls=%fused_computation.12 | convolution fusion | flops 4836950016 | bytes 14942208 | tf_op jit(solution)/shard_map/dot_general | solution.py:18
  140.2 6.3 %reshape.315 = bf16[128,6,2048]{2,1,0:T(8,128)(2,1)} reshape(bf16[768,2048]{1,0:T(8,128)(2,1)} %convolution_convert_fusion) | data formatting | bytes 6291456 | tf_op jit(solution)/shard_map/reshape | solution.py:19
  146.5 0.0 all-to-all-done
  146.5 10.5 %all-to-all-start.3 = ((bf16[128,6,2048]{2,1,0:T(8,128)(2,1)}), bf16[128,6,2048]{2,1,0:T(8,128)(2,1)}, u32[]{:S(2)}, u32[]{:S(2)}) async-start(bf16[128,6,2048]{2,1,0:T(8,128)(2,1)} %reshape.315), calls=%async_computation.3 | async-start | bytes 8388608 | tf_op jit(solution)/shard_map/all_to_all | solution.py:84
  157.0 152.7 %all-reduce.3.cloned.1.call-done = (bf16[768,2048]{1,0:T(8,128)(2,1)}, bf16[2048,768]{1,0:T(8,128)(2,1)}, bf16[2048,768]{1,0:T(8,128)(2,1)}) async-done(((bf16[768,2048]{1,0:T(8,128)(2,1)}, bf16[2048,768]{1,0:T(8,128)(2,1)}, bf16[2048,768]{1,0:T(8,128)(2,1)}), (bf16[768,2048]{1,0:T(8,128)(2,1)}, bf16[2048,768]{1,0:T(8,128)(2,1)}, bf16[2048,768]{1,0:T(8,128)(2,1)})) %all-reduce.3.cloned.1.call-update) | async-done | bytes 9437200 | tf_op jit(solution)/shard_map/psum | solution.py:9
  309.7 4.8 fusion.31
  314.5 8.6 %convolution_convert_fusion.1 = bf16[512,2048]{1,0:T(8,128)(2,1)} fusion(bf16[768,2048]{1,0:T(8,128)(2,1)} %get-tuple-element.5, f32[512,768]{1,0:T(8,128)} %fusion.31, bf16[512,2048]{1,0:T(8,128)(2,1)S(1)} %bitcast.53, bf16[2048,768]{1,0:T(8,128)(2,1)} %get-tuple-element.7), kind=kOutput, calls=%fused_computation.21 | convolution fusion | flops 3224633344 | bytes 12058624 | tf_op jit(solution)/shard_map/dot_general | solution.py:18
  323.1 0.0 all-to-all-done.3
  323.2 9.7 %all-to-all-start.1 = ((bf16[32,16,2048]{2,1,0:T(8,128)(2,1)}), bf16[32,16,2048]{2,1,0:T(8,128)(2,1)S(1)}, u32[]{:S(2)}, u32[]{:S(2)}) async-start(bf16[32,16,2048]{2,1,0:T(8,128)(2,1)} %bitcast.51), calls=%async_computation.1 | async-start | bytes 4194304 | tf_op jit(solution)/shard_map/all_to_all | solution.py:75
  332.9 0.1 gt.32
  333.0 0.0 copy-done.4
  333.0 0.1 copy.18
  333.2 0.1 broadcast_select_fusion.2
  333.2 27.9 %psum.38 = s32[4,128]{0,1:T(8,128)S(1)} all-reduce(s32[4,128]{0,1:T(8,128)S(1)} %broadcast_select_fusion.2), channel_id=1, replica_groups=mesh['rep'=4,'ep'=32] {'rep'}, use_global_device_ids=true, to_apply=%region_15.16 | all-reduce | flops 512 | bytes 4096 | tf_op jit(solution)/shard_map/psum | solution.py:40
  361.1 185.7 %psum.39 = s32[4,128]{0,1:T(8,128)S(1)} all-reduce(s32[4,128]{0,1:T(8,128)S(1)} %psum.38), channel_id=1, replica_groups=mesh['rep'=4,'ep'=32] {'ep'}, use_global_device_ids=true, to_apply=%region_16.17 | all-reduce | flops 512 | bytes 4096 | tf_op jit(solution)/shard_map/psum | solution.py:40
  546.8 0.1 reduce_sum.62
  546.9 0.6 gather_fusion.4
  547.5 0.1 copy.24
  547.6 0.1 reshape.317
  547.7 0.5 convert_multiply_fusion
  548.2 6.3 %reshape.316 = bf16[768,2048]{1,0:T(8,128)(2,1)} reshape(bf16[128,6,2048]{2,1,0:T(8,128)(2,1)} %all-to-all-done.3) | data formatting | bytes 6291456 | tf_op jit(solution)/shard_map/reshape | solution.py:85
  554.5 11.1 %gather_fusion.3 = bf16[1024,2048]{1,0:T(8,128)(2,1)} fusion(bf16[768,2048]{1,0:T(8,128)(2,1)} %reshape.316, s32[1024]{0:T(1024)S(1)} %broadcast_clamp_fusion), kind=kCustom, calls=%fused_computation.3 | custom fusion | bytes 8392704 | tf_op jit(solution)/shard_map/gather | solution.py:85
  565.6 0.0 all-to-all-done.1
  565.7 6.0 %gather_fusion.1 = bf16[1024,2048]{1,0:T(8,128)(2,1)} fusion(bf16[512,2048]{1,0:T(8,128)(2,1)S(1)} %bitcast.49, s32[1024]{0:T(1024)S(1)} %broadcast_clamp_fusion.1), kind=kCustom, calls=%fused_computation.1 | custom fusion | bytes 8392704 | tf_op jit(solution)/shard_map/gather | solution.py:76
  571.7 7.0 %multiply_reduce_fusion = bf16[128,2048]{1,0:T(8,128)(2,1)} fusion(bf16[1024,2048]{1,0:T(8,128)(2,1)} %gather_fusion.3, bf16[1024,2048]{1,0:T(8,128)(2,1)} %gather_fusion.1, f32[128,8]{1,0:T(8,128)S(1)} %copy.18, pred[128,8]{1,0:T(8,128)(4,1)S(1)} %gt.32), kind=kLoop, calls=%fused_computation.9 | loop fusion | flops 8126464 | bytes 8918016 | tf_op jit(solution)/shard_map/reduce_sum | solution.py:88
  578.7 0.0 copy-done.1
  (28 shorter events, 0.2 us)
Async XLA Ops:
  7.2 16.6 %copy-start = (bf16[128,2048]{1,0:T(8,128)(2,1)S(1)}, bf16[128,2048]{1,0:T(8,128)(2,1)}, u32[]{:S(2)}) copy-start(bf16[128,2048]{1,0:T(8,128)(2,1)} %param.7) | copy-start | bytes 1572868
  7.2 302.5 %all-reduce.3.cloned.1.call-start = ((), (), s32[]{:S(2)}) async-start(), calls=%async_computation.4 | async-start | bytes 18874368 | tf_op jit(solution)/shard_map/psum | solution.py:9
  9.2 3.9 copy-start.2
  9.2 4.9 copy-start.3
  17.1 0.7 copy-start.5
  17.1 1.6 copy-start.6
  43.7 62.6 %all-to-all-start.2 = ((bf16[128,6,2048]{2,1,0:T(8,128)(2,1)}), bf16[128,6,2048]{2,1,0:T(8,128)(2,1)}, u32[]{:S(2)}, u32[]{:S(2)}) async-start(bf16[128,6,2048]{2,1,0:T(8,128)(2,1)} %broadcast_select_fusion), calls=%async_computation.2 | async-start | bytes 8388608 | tf_op jit(solution)/shard_map/all_to_all | solution.py:79
  106.3 40.2 %all-to-all-start = ((bf16[32,16,2048]{2,1,0:T(8,128)(2,1)}), bf16[32,16,2048]{2,1,0:T(8,128)(2,1)S(1)}, u32[]{:S(2)}, u32[]{:S(2)}) async-start(bf16[32,16,2048]{2,1,0:T(8,128)(2,1)} %broadcast_select_fusion.1), calls=%async_computation | async-start | bytes 4194304 | tf_op jit(solution)/shard_map/all_to_all | solution.py:70
  146.5 176.7 %all-to-all-start.3 = ((bf16[128,6,2048]{2,1,0:T(8,128)(2,1)}), bf16[128,6,2048]{2,1,0:T(8,128)(2,1)}, u32[]{:S(2)}, u32[]{:S(2)}) async-start(bf16[128,6,2048]{2,1,0:T(8,128)(2,1)} %reshape.315), calls=%async_computation.3 | async-start | bytes 8388608 | tf_op jit(solution)/shard_map/all_to_all | solution.py:84
  323.1 9.9 %copy-start.4 = (f32[128,8]{0,1:T(8,128)S(1)}, f32[128,8]{0,1:T(8,128)}, u32[]{:S(2)}) copy-start(f32[128,8]{0,1:T(8,128)} %param.9) | copy-start | bytes 12292
  323.2 242.5 %all-to-all-start.1 = ((bf16[32,16,2048]{2,1,0:T(8,128)(2,1)}), bf16[32,16,2048]{2,1,0:T(8,128)(2,1)S(1)}, u32[]{:S(2)}, u32[]{:S(2)}) async-start(bf16[32,16,2048]{2,1,0:T(8,128)(2,1)} %bitcast.51), calls=%async_computation.1 | async-start | bytes 4194304 | tf_op jit(solution)/shard_map/all_to_all | solution.py:75
  565.6 13.0 %copy-start.1 = (bf16[128,2048]{1,0:T(8,128)(2,1)S(1)}, bf16[128,2048]{1,0:T(8,128)(2,1)}, u32[]{:S(2)}) copy-start(bf16[128,2048]{1,0:T(8,128)(2,1)} %param.7) | copy-start | bytes 1572868
Sparse Core Ops, SparseCore 0:
  17.3 292.3 all-reduce.2
